TPU v7x, 32 devices: a whole 2x2x4 slice. The times are simulated.
32 devices in a mesh: rows: 4 (over y, x), grid: 8 (over z, core).
Axes of the slice: x: 2, y: 2, z: 4, core: 2. Of those that a mesh axis runs over, the one named last changes fastest.
Arguments:
- positions: int32 [2, 2048], P(None, 'rows'), may hold values from 0 to 63, as said below
- angles: int32 [2, 4096], P(None, 'grid'), may hold values from 0 to 4095
- subspace: bfloat16 [2, 2048, 1920], P(None, 'rows', 'grid')
Outputs:
- spectrum: float32 [4096], P('grid')
Inputs may be any that keep to these rules, and one draw needn't show every extreme that they name: `positions`: each column names a distinct lattice point; both coordinates lie in 0 to 63.
All inputs are finite; a program needn't handle non-finite values.
Results may differ from a plain program's by a relative error of at most 0.0012.
Values may be sent and summed in bfloat16 or wider, within the bound.
A program may use at most 64 MiB of HBM per device.

v0:
```python
import math

import jax
import jax.numpy as jnp
from jax import lax
from jax.sharding import PartitionSpec as P

NOISE = 1920
PHASES = 4096


def steering_block(positions, angle_block):
    phase_index = (
        positions[0][:, None] * angle_block[0][None, :]
        + positions[1][:, None] * angle_block[1][None, :]
    ) % PHASES
    phase = phase_index.astype(jnp.float32) * (2.0 * math.pi / PHASES)
    return jnp.concatenate([jnp.cos(phase), jnp.sin(phase)], 0).astype(jnp.bfloat16)


def project_with(column_piece, steering):
    real_part = column_piece[0]
    imag_part = column_piece[1]
    upper_half = jnp.concatenate([real_part, imag_part], 0)
    lower_half = jnp.concatenate([-imag_part, real_part], 0)
    stacked = jnp.stack([upper_half, lower_half])
    return jnp.einsum("pmk,ma->pka", stacked, steering, preferred_element_type=jnp.float32)


def body(positions, angles, subspace):
    whole_columns = lax.all_gather(subspace, "grid", axis=2, tiled=True)
    column_share = lax.all_to_all(whole_columns, "rows", split_axis=2, concat_axis=1, tiled=True)
    all_positions = lax.all_gather(positions, "rows", axis=1, tiled=True)
    steering = steering_block(all_positions, angles)
    projected = project_with(column_share, steering)
    squares = lax.psum(jnp.sum(projected * projected, axis=(0, 1)), "rows")
    return 1.0 / (squares / NOISE + 1e-06)


def solution(mesh):
    in_specs = (P(None, "rows"), P(None, "grid"), P(None, "rows", "grid"))
    out_specs = P("grid")
    return jax.shard_map(body, mesh=mesh, in_specs=in_specs, out_specs=out_specs, check_vma=False)
```

profile of v0, /device:TPU:0, one launch (start us, length us, event | category | flops | bytes accessed | tf_op | source)
XLA Modules:
  0.0 159.4 jit_solution(3031603757623284089)
XLA Ops:
  6.5 0.0 all-gather.2.cloned.1.call-start
  6.5 2.3 %copy.7 = bf16[2,512,240]{1,0,2:T(2,128)(2,1)} copy(bf16[2,512,240]{1,2,0:T(8,128)(2,1)} %param.5) | data formatting | bytes 983040 | tf_op args[2]
  8.8 0.0 all-gather.2.cloned.1.call-update
  8.9 0.0 copy-start.1
  8.9 0.0 copy-start.2
  8.9 47.6 %all-gather.2.cloned.1.call-done = bf16[2,512,1920]{1,0,2:T(2,128)(2,1)} async-done(((bf16[2,512,240]{1,0,2:T(2,128)(2,1)}), bf16[2,512,1920]{1,0,2:T(2,128)(2,1)}) %all-gather.2.cloned.1.call-update) | async-done | bytes 3932176 | tf_op jit(solution)/shard_map/all_gather | solution.py:31
  56.5 4.8 %all-to-all-start = ((bf16[2,512,1920]{1,0,2:T(2,128)(2,1)}), bf16[2,512,1920]{1,0,2:T(2,128)(2,1)}, u32[]{:S(2)}, u32[]{:S(2)}) async-start(bf16[2,512,1920]{1,0,2:T(2,128)(2,1)} %all-gather.2.cloned.1.call-done), calls=%async_computation | async-start | bytes 7864320 | tf_op jit(solution)/shard_map/all_to_all | solution.py:32
  61.2 0.0 copy-done.1
  61.3 46.9 %all_gather.7 = s32[2,2048]{1,0:T(2,128)S(1)} all-gather(s32[2,512]{1,0:T(2,128)S(1)} %copy-done.1), channel_id=1, replica_groups=mesh['rows'=4,'grid'=8] {'rows'}, dimensions={1}, use_global_device_ids=true | all-gather | bytes 20480 | tf_op jit(solution)/shard_map/all_gather | solution.py:33
  108.1 0.0 copy-done.2
  108.1 19.3 %cosine_convert_fusion = (bf16[2048,512]{1,0:T(8,128)(2,1)S(1)}, bf16[2048,512]{1,0:T(8,128)(2,1)}) fusion(s32[512]{0:T(512)S(1)} %bitcast.36, s32[2048]{0:T(1024)S(1)} %bitcast.34, s32[512]{0:T(512)S(1)} %bitcast.35, s32[2048]{0:T(1024)S(1)} %bitcast.33), kind=kLoop, calls=%fused_computation.14 | loop fusion | flops 18874368 | bytes 4214784 | tf_op jit(solution)/shard_map/convert
  127.5 0.0 all-to-all-done
  127.5 5.1 %copy.12 = bf16[2,512,4,480]{1,2,3,0:T(4,128)(2,1)S(1)} copy(bf16[2,512,4,480]{1,0,3,2:T(2,128)(2,1)} %bitcast) | data formatting | bytes 7864320 | tf_op jit(solution)/shard_map/all_to_all | solution.py:32
  132.6 1.4 fusion.12
  134.0 0.6 copy.10
  134.6 0.5 neg.3
  135.1 0.6 copy.9
  135.7 0.0 copy-start
  135.7 0.9 maximum_bitcast_fusion.2
  136.6 0.6 copy-done
  137.3 4.2 %multiply_reduce_fusion = f32[512]{0:T(512)S(1)} fusion(bf16[2048,512]{1,0:T(8,128)(2,1)S(1)} %copy-done, bf16[2048,512]{1,0:T(8,128)(2,1)S(1)} %get-tuple-element.9, bf16[1,4096,480]{1,2,0:T(8,128)(2,1)S(1)} %get-tuple-element.8, bf16[1,4096,480]{1,2,0:T(8,128)(2,1)S(1)} %get-tuple-element.7), kind=kOutput, calls=%fused_computation.18 | convolution fusion | flops 4039835136 | bytes 12060672 | tf_op jit(solution)/shard_map/pmk,ma->pka/dot_general | solution.py:27
  141.5 10.5 %psum.7 = f32[512]{0:T(512)S(1)} all-reduce(f32[512]{0:T(512)S(1)} %multiply_reduce_fusion), channel_id=1, replica_groups=mesh['rows'=4,'grid'=8] {'rows'}, use_global_device_ids=true, to_apply=%region_1.2 | all-reduce | flops 512 | bytes 4096 | tf_op jit(solution)/shard_map/psum | solution.py:36
  152.0 0.6 add_divide_fusion
  (2 shorter events, 0.0 us)
Async XLA Ops:
  6.5 49.9 %all-gather.2.cloned.1.call-start = ((), (), s32[]{:S(2)}) async-start(), calls=%async_computation.1 | async-start | bytes 4423680 | tf_op jit(solution)/shard_map/all_gather | solution.py:31
  8.9 52.4 %copy-start.1 = (s32[2,512]{1,0:T(2,128)S(1)}, s32[2,512]{1,0:T(2,128)}, u32[]{:S(2)}) copy-start(s32[2,512]{1,0:T(2,128)} %param.3) | copy-start | bytes 12292
  8.9 99.2 %copy-start.2 = (s32[2,512]{1,0:T(2,128)S(1)}, s32[2,512]{1,0:T(2,128)}, u32[]{:S(2)}) copy-start(s32[2,512]{1,0:T(2,128)} %param.4) | copy-start | bytes 12292
  56.5 71.0 %all-to-all-start = ((bf16[2,512,1920]{1,0,2:T(2,128)(2,1)}), bf16[2,512,1920]{1,0,2:T(2,128)(2,1)}, u32[]{:S(2)}, u32[]{:S(2)}) async-start(bf16[2,512,1920]{1,0,2:T(2,128)(2,1)} %all-gather.2.cloned.1.call-done), calls=%async_computation | async-start | bytes 7864320 | tf_op jit(solution)/shard_map/all_to_all | solution.py:32
  135.7 1.6 %copy-start = (bf16[2048,512]{1,0:T(8,128)(2,1)S(1)}, bf16[2048,512]{1,0:T(8,128)(2,1)}, u32[]{:S(2)}) copy-start(bf16[2048,512]{1,0:T(8,128)(2,1)} %get-tuple-element.10) | copy-start | bytes 6291460
Sparse Core Ops, SparseCore 0:
  9.0 47.4 all-gather.1
where the time goes:
time: 160 us; the launch traced here: 159 us
  blocking collectives  57.3 us (36%)
  waiting for transfers between devices  47.6 us (30%)
  other arithmetic  21.3 us (13%)
  between operations  13.5 us (8%)
  local copies, waits for them, and re-layouts  10.7 us (7%)
  starting transfers between devices  4.79 us (3%)
  matrix products  4.22 us (3%)
    all_gather x1, waiting for transfers between devices, body(): whole_columns = lax.all_gather(subspace, 'grid', axis=2, tiled=True)  47.6 us
    all_gather x1, blocking collectives, body(): all_positions = lax.all_gather(positions, 'rows', axis=1, tiled=True)  46.9 us
    another operation x1, other arithmetic  19.3 us
    psum x1, blocking collectives, body(): squares = lax.psum(jnp.sum(projected * projected, axis=(0, 1)), 'rows')  10.5 us
    all_to_all x1, local copies, waits for them, and re-layouts, body(): lax.all_to_all(whole_columns, 'rows', split_axis=2, concat_axis=1, tiled=...  5.15 us
    all_to_all x1, starting transfers between devices, body(): lax.all_to_all(whole_columns, 'rows', split_axis=2, concat_axis=1, tiled=...  4.79 us
    dot_general x1, matrix products, project_with(): jnp.einsum('pmk,ma->pka', stacked, steering, preferred_element_type=jnp.f...  4.22 us
    unnamed x9, local copies, waits for them, and re-layouts  4.11 us
  transfers between devices with their start and end apart: 2, of which 1 were waited for; matrix products, arithmetic and copies ran while one was open for 12% of the time, Pallas kernels for 0%

commit v1 on v0

v1 whole, which is shorter than its diff:
```python
import functools

import jax
import jax.numpy as jnp
from jax import lax
from jax.experimental import pallas as pl
from jax.experimental.pallas import tpu as pltpu
from jax.sharding import PartitionSpec as P

PHASES = 4096
LOADING = 1e-06
MESH = pl.DeviceIdType.MESH
LANES = 128
TILE = 256
CHUNK = 64

COS_ODD = (-6.283164024353027, 41.33714294433594, -81.34076690673828, 70.9933853149414)
SIN_EVEN = (
    0.9999999403953552,
    -19.739171981811523,
    64.9345932006836,
    -85.24032592773438,
    56.242347717285156,
)


def horner(coefficients, x):
    total = coefficients[-1] * x + coefficients[-2]
    for c in coefficients[-3::-1]:
        total = total * x + c
    return total


def cos_sin(turns):
    r = turns - jnp.round(turns)
    w = jnp.abs(r) - 0.25
    w2 = w * w
    cos = horner(COS_ODD, w2) * w
    sin = horner(SIN_EVEN, w2)
    return cos, jnp.where(r < 0.0, -sin, sin)


def flip(bit, by):
    return 1 - bit if by else bit


def kernel(
    rows, grid, noise, pos_ref, ang_ref, v_ref, out_ref,
    pos, ang, acol, v, lhs_a, lhs_b, acc, part, red,
    ang_send, ang_recv, pos_send, pos_recv, own_sem,
    row_send, row_recv, core_send, core_recv, red_send, red_recv,
):
    r, g = lax.axis_index("rows"), lax.axis_index("grid")
    half, y = r % 2, r // 2
    core, chip = g % 2, g // 2
    blocks = grid // 4
    group = y * 2 + core
    per_block = ang_ref.shape[1]
    elements = pos_ref.shape[1]
    tiles = blocks * per_block // TILE

    def row_partner(j):
        return flip(y, j // 2) * 2 + flip(half, j % 2)

    barrier = pltpu.get_barrier_semaphore()
    for j in range(1, 4):
        pl.semaphore_signal(barrier, inc=1, device_id=(row_partner(j), g), device_id_type=MESH)

    def greet(d, carry):
        pl.semaphore_signal(barrier, inc=1, device_id=(r, (g + d) % grid), device_id_type=MESH)
        return carry

    lax.fori_loop(1, grid, greet, 0)
    pl.semaphore_wait(barrier, 3 + grid - 1)

    pos_copies = []
    for j in range(1, 4):
        pos_copies.append(pltpu.make_async_remote_copy(
            pos_ref, pos.at[j], pos_send.at[j], pos_recv.at[j],
            device_id=(row_partner(j), g), device_id_type=MESH))
        pos_copies[-1].start()

    def send_angles(d, carry):
        pltpu.make_async_remote_copy(
            ang_ref, ang.at[g], ang_send, ang_recv,
            device_id=(r, (g + d) % grid), device_id_type=MESH).start()
        return carry

    lax.fori_loop(1, grid, send_angles, 0)
    pltpu.make_async_copy(ang_ref, ang.at[g], ang_recv).start()

    row_copies = []
    for j in range(1, 4):
        row_copies.append(pltpu.make_async_remote_copy(
            v_ref.at[flip(half, j % 2)], v.at[j, core], row_send.at[j], row_recv.at[j],
            device_id=(row_partner(j), g), device_id_type=MESH))

    def core_copy(j, source):
        return pltpu.make_async_remote_copy(
            source, v.at[j, core], core_send.at[j], core_recv.at[j],
            device_id=(r, chip * 2 + 1 - core), device_id_type=MESH)

    core_copies = [core_copy(0, v_ref.at[half])] + [core_copy(j, v.at[j, core]) for j in range(1, 4)]
    core_copies[0].start()
    own_copy = pltpu.make_async_copy(v_ref.at[half], v.at[0, core], own_sem)
    own_copy.start()
    for copy in row_copies:
        copy.start()

    pos[0] = pos_ref[...]
    pltpu.make_async_copy(ang, ang, ang_recv).wait()
    for i in range(blocks):
        for k in range(2):
            line = ang[group * blocks + i, k : k + 1, :].astype(jnp.float32) * (1.0 / PHASES)
            acol[k, i * per_block : (i + 1) * per_block, :] = jnp.broadcast_to(line, (LANES, per_block)).T
    for copy in pos_copies:
        copy.wait_recv()

    def steer(step, lhs):
        j, tile = step // tiles, step % tiles
        p = pos[j].astype(jnp.float32)
        start = pl.multiple_of(tile * TILE, TILE)
        for row in range(0, TILE, CHUNK):
            a0 = acol[0, pl.ds(start + row, CHUNK), :]
            a1 = acol[1, pl.ds(start + row, CHUNK), :]
            for lane in range(0, elements, LANES):
                turns = a0 * p[0:1, lane : lane + LANES] + a1 * p[1:2, lane : lane + LANES]
                cos, sin = cos_sin(turns)
                cos, sin = cos.astype(jnp.bfloat16), sin.astype(jnp.bfloat16)
                lhs[row : row + CHUNK, lane : lane + LANES] = cos
                lhs[row : row + CHUNK, elements + lane : elements + lane + LANES] = sin
                lhs[TILE + row : TILE + row + CHUNK, lane : lane + LANES] = sin
                lhs[TILE + row : TILE + row + CHUNK, elements + lane : elements + lane + LANES] = -cos

    width = v.shape[-1]

    def project(j, tile, lhs):
        columns = jnp.concatenate(
            [v[j, 0].reshape(2 * elements, width), v[j, 1].reshape(2 * elements, width)], 1)
        product = jnp.dot(lhs[...], columns, preferred_element_type=jnp.float32)
        if j == 0:
            acc[tile] = product
        else:
            acc[tile] += product

    last = 4 * tiles - 1

    def run(j):
        @pl.loop(0, tiles // 2)
        def _(pair):
            step = j * tiles + 2 * pair
            steer(step + 1, lhs_b)
            project(j, 2 * pair, lhs_a)
            steer(jnp.minimum(step + 2, last), lhs_a)
            project(j, 2 * pair + 1, lhs_b)

    steer(0, lhs_a)
    own_copy.wait()
    core_copies[0].wait_recv()
    run(0)
    for j in (1, 2):
        row_copies[j - 1].wait_recv()
        core_copies[j].start()
    core_copies[1].wait_recv()
    run(1)
    row_copies[2].wait_recv()
    core_copies[3].start()
    core_copies[2].wait_recv()
    run(2)
    core_copies[3].wait_recv()
    run(3)

    for tile in range(tiles):
        sums = acc[tile, 0:TILE] * acc[tile, 0:TILE] + acc[tile, TILE:] * acc[tile, TILE:]
        folded = sums[:, 0:LANES]
        for lane in range(LANES, sums.shape[1], LANES):
            folded = folded + sums[:, lane : lane + LANES]
        offset = tile * TILE % per_block
        part[tile * TILE // per_block, :, offset : offset + TILE] = jnp.sum(folded.T, axis=0, keepdims=True)

    slot = half * (grid // 2) + chip
    transfers = []
    for i in range(blocks):
        for row in range(4):
            target = group * blocks + i
            here = jnp.logical_and(target == g, r == row)
            index = i * 4 + row
            remote = pltpu.make_async_remote_copy(
                part.at[i], red.at[slot], red_send.at[index], red_recv.at[slot],
                device_id=(row, target), device_id_type=MESH)
            local = pltpu.make_async_copy(part.at[i], red.at[slot], red_recv.at[slot])
            transfers.append((here, remote))
            pl.when(here)(local.start)
            pl.when(jnp.logical_not(here))(remote.start)
    for s in range(grid):
        pltpu.make_async_copy(part.at[0], red.at[s], red_recv.at[s]).wait()
    squares = red[0]
    for s in range(1, grid):
        squares = squares + red[s]
    out_ref[...] = 1.0 / (squares / noise + LOADING)

    for here, remote in transfers:
        pl.when(jnp.logical_not(here))(remote.wait_send)
    for copy in pos_copies + row_copies + core_copies:
        copy.wait_send()
    others = ang.at[pl.ds(0, grid - 1)]
    pltpu.make_async_copy(others, others, ang_send).wait()


def body(rows, grid, positions, angles, subspace):
    parts, elements, columns = subspace.shape
    width = LANES * pl.cdiv(pl.cdiv(columns, 2), LANES)
    padded = jnp.pad(subspace, ((0, 0), (0, 0), (0, 2 * width - columns)))
    halves = jnp.moveaxis(padded.reshape(parts, elements, 2, width), 2, 0)
    per_block = angles.shape[1]
    blocks = grid // 4
    group_angles = blocks * per_block
    tiles = group_angles // TILE
    noise = columns * grid
    dma = pltpu.SemaphoreType.DMA
    out = pl.pallas_call(
        functools.partial(kernel, rows, grid, noise),
        out_shape=jax.ShapeDtypeStruct((1, per_block), jnp.float32),
        in_specs=[
            pl.BlockSpec(memory_space=pltpu.VMEM),
            pl.BlockSpec(memory_space=pltpu.VMEM),
            pl.BlockSpec(memory_space=pl.ANY),
        ],
        out_specs=pl.BlockSpec(memory_space=pltpu.VMEM),
        scratch_shapes=[
            pltpu.VMEM((4, 2, elements), jnp.int32),
            pltpu.VMEM((grid, 2, per_block), jnp.int32),
            pltpu.VMEM((2, group_angles, LANES), jnp.float32),
            pltpu.VMEM((4, 2, 2, elements, width), jnp.bfloat16),
            pltpu.VMEM((2 * TILE, 2 * elements), jnp.bfloat16),
            pltpu.VMEM((2 * TILE, 2 * elements), jnp.bfloat16),
            pltpu.VMEM((tiles, 2 * TILE, 2 * width), jnp.float32),
            pltpu.VMEM((blocks, 1, per_block), jnp.float32),
            pltpu.VMEM((grid, 1, per_block), jnp.float32),
            dma, dma, dma((4,)), dma((4,)), dma,
            dma((4,)), dma((4,)), dma((4,)), dma((4,)), dma((4 * blocks,)), dma((grid,)),
        ],
        compiler_params=pltpu.CompilerParams(collective_id=0, has_side_effects=True),
    )(positions, angles, halves)
    return out.reshape(per_block)


def solution(mesh):
    rows, grid = mesh.shape["rows"], mesh.shape["grid"]
    in_specs = (P(None, "rows"), P(None, "grid"), P(None, "rows", "grid"))
    fn = functools.partial(body, rows, grid)
    return jax.shard_map(fn, mesh=mesh, in_specs=in_specs, out_specs=P("grid"), check_vma=False)
```

time: 160 us -> 34.3 us (0.21)
  blocking collectives: 57.3 us -> 0 us
  waiting for transfers between devices: 47.6 us -> 0 us
  Pallas kernels: 0 us -> 30.7 us
  other arithmetic: 21.3 us -> 0 us
  between operations: 13.5 us -> 0.01 us
  local copies, waits for them, and re-layouts: 10.7 us -> 3.32 us
  starting transfers between devices: 4.79 us -> 0 us
  matrix products: 4.22 us -> 0 us
    all_gather x1 -> x0, waiting for transfers between devices: 47.6 us -> none  [body(): whole_columns = lax.all_gather(subspace, 'grid', axis=2, tiled=True)]
    all_gather x1 -> x0, blocking collectives: 46.9 us -> none  [body(): all_positions = lax.all_gather(positions, 'rows', axis=1, tiled=True)]
    pallas_call x0 -> x1, Pallas kernels: none -> 30.7 us  [body(): pl.pallas_call(functools.partial(kernel, rows, grid, noise), out_shape=ja...]
    another operation x2 -> x0, other arithmetic: 20.3 us -> none
    psum x1 -> x0, blocking collectives: 10.5 us -> none  [body(): squares = lax.psum(jnp.sum(projected * projected, axis=(0, 1)), 'rows')]
    all_to_all x1 -> x0, local copies, waits for them, and re-layouts: 5.15 us -> none  [body(): lax.all_to_all(whole_columns, 'rows', split_axis=2, concat_axis=1, tiled=...]
    all_to_all x1 -> x0, starting transfers between devices: 4.79 us -> none  [body(): lax.all_to_all(whole_columns, 'rows', split_axis=2, concat_axis=1, tiled=...]
    dot_general x1 -> x0, matrix products: 4.22 us -> none  [project_with(): jnp.einsum('pmk,ma->pka', stacked, steering, preferred_element_type=jnp.f...]
  transfers between devices with their start and end apart: 2 -> 0, of which waited for: 1 -> 0; matrix products, arithmetic and copies ran while one was open for 12% -> 0% of each run, Pallas kernels for 0% -> 0%
where the time goes in v1:
time: 34.3 us; the launch traced here: 34.1 us
  Pallas kernels  30.7 us (90%)
  local copies, waits for them, and re-layouts  3.32 us (10%)
    pallas_call x1, Pallas kernels, body(): pl.pallas_call(functools.partial(kernel, rows, grid, noise), out_shape=ja...  30.7 us
    unnamed x1, local copies, waits for them, and re-layouts  1.26 us
    pad x1, local copies, waits for them, and re-layouts, body(): padded = jnp.pad(subspace, ((0, 0), (0, 0), (0, 2 * width - columns)))  1.06 us
    reshape x1, local copies, waits for them, and re-layouts, body(): halves = jnp.moveaxis(padded.reshape(parts, elements, 2, width), 2, 0)  1 us

profile of v1, /device:TPU:0, one launch (start us, length us, event | category | flops | bytes accessed | tf_op | source)
XLA Modules:
  0.0 34.1 jit_solution(11141037439613768901)
XLA Ops:
  0.0 1.1 %pad.4 = bf16[2,512,256]{1,2,0:T(8,128)(2,1)S(1)} pad(bf16[2,512,240]{1,2,0:T(8,128)(2,1)} %param.5, bf16[]{:T(256)} %constant.2.clone.1), padding=0_0x0_0x0_16 | pad | bytes 1015810 | tf_op jit(solution)/shard_map/jit(_pad)/pad | solution.py:213
  1.1 1.0 %copy.4 = bf16[2,512,2,128]{3,1,0,2:T(8,128)(2,1)} copy(bf16[2,512,2,128]{1,3,2,0:T(8,128)(2,1)S(1)} %bitcast.3) | data formatting | bytes 1048576 | tf_op jit(solution)/shard_map/reshape | solution.py:214
  2.1 30.7 %shard_map.37 = f32[1,512]{1,0:T(1,128)} custom-call(s32[2,512]{1,0:T(2,128)} %pos_ref.1, s32[2,512]{1,0:T(2,128)} %ang_ref.1, bf16[2,2,512,128]{3,2,1,0:T(8,128)(2,1)} %bitcast.4), custom_call_target="tpu_custom_call" | custom-call | tf_op jit(solution)/shard_map/pallas_call | solution.py:221
  32.8 1.3 %copy.6 = f32[512]{0:T(512)} copy(f32[512]{0:T(512)} %bitcast.5) | data formatting | bytes 4096

commit v2 on v1

v2 whole, which is shorter than its diff:
```python
import functools

import jax
import jax.numpy as jnp
from jax import lax
from jax.experimental import pallas as pl
from jax.experimental.pallas import tpu as pltpu
from jax.sharding import PartitionSpec as P

PHASES = 4096
LOADING = 1e-06
MESH = pl.DeviceIdType.MESH
LANES = 128
SUBLANES = 16
TILE = 256
CHUNK = 32
SPAN = 2

COS_ODD = (-6.283164024353027, 41.33714294433594, -81.34076690673828, 70.9933853149414)
SIN_EVEN = (
    0.9999999403953552,
    -19.739171981811523,
    64.9345932006836,
    -85.24032592773438,
    56.242347717285156,
)


def horner(coefficients, x):
    total = coefficients[-1] * x + coefficients[-2]
    for c in coefficients[-3::-1]:
        total = total * x + c
    return total


def cos_sin(turns):
    r = turns - jnp.round(turns)
    w = jnp.abs(r) - 0.25
    w2 = w * w
    cos = horner(COS_ODD, w2) * w
    sin = horner(SIN_EVEN, w2)
    return cos, jnp.where(r < 0.0, -sin, sin)


def flip(bit, by):
    return 1 - bit if by else bit


def kernel(
    grid, noise, pos_ref, ang_ref, v_ref, out_ref,
    pos, ang, pcol, v, steering, acc, part, red,
    ang_send, ang_recv, pos_send, pos_recv, own_sem,
    row_send, row_recv, core_send, core_recv, red_send, red_recv,
):
    r, g = lax.axis_index("rows"), lax.axis_index("grid")
    half, y = r % 2, r // 2
    core, chip = g % 2, g // 2
    blocks = grid // 4
    group = y * 2 + core
    per_block = ang_ref.shape[1]
    elements = pos_ref.shape[1]
    width = v.shape[3]
    stored = v_ref.shape[1]
    shared = 2 * width - stored
    angles = steering.shape[2] // 2

    def row_partner(j):
        return flip(y, j // 2) * 2 + flip(half, j % 2)

    barrier = pltpu.get_barrier_semaphore()
    for j in range(1, 4):
        pl.semaphore_signal(barrier, inc=1, device_id=(row_partner(j), g), device_id_type=MESH)

    def greet(d, carry):
        pl.semaphore_signal(barrier, inc=1, device_id=(r, (g + d) % grid), device_id_type=MESH)
        return carry

    lax.fori_loop(1, grid, greet, 0)
    pl.semaphore_wait(barrier, 3 + grid - 1)

    pos_copies = []
    for j in range(1, 4):
        pos_copies.append(pltpu.make_async_remote_copy(
            pos_ref, pos.at[j], pos_send.at[j], pos_recv.at[j],
            device_id=(row_partner(j), g), device_id_type=MESH))
        pos_copies[-1].start()

    def send_angles(d, carry):
        pltpu.make_async_remote_copy(
            ang_ref, ang.at[g], ang_send, ang_recv,
            device_id=(r, (g + d) % grid), device_id_type=MESH).start()
        return carry

    lax.fori_loop(1, grid, send_angles, 0)
    pltpu.make_async_copy(ang_ref, ang.at[g], ang_recv).start()

    def share(which):
        return v_ref.at[:, pl.ds(pl.multiple_of(which * (stored - width), SUBLANES), width), :]

    row_copies = []
    for j in range(1, 4):
        row_copies.append(pltpu.make_async_remote_copy(
            share(flip(half, j % 2)), v.at[j, core], row_send.at[j], row_recv.at[j],
            device_id=(row_partner(j), g), device_id_type=MESH))

    def core_copy(j, source):
        return pltpu.make_async_remote_copy(
            source, v.at[j, core], core_send.at[j], core_recv.at[j],
            device_id=(r, chip * 2 + 1 - core), device_id_type=MESH)

    core_copies = [core_copy(0, share(half))] + [core_copy(j, v.at[j, core]) for j in range(1, 4)]
    row_copies[0].start()
    row_copies[1].start()
    core_copies[0].start()
    own_copy = pltpu.make_async_copy(share(half), v.at[0, core], own_sem)
    own_copy.start()

    def spread_positions(j):
        for k in range(2):
            line = (pos_ref[k : k + 1, :] if j == 0 else pos[j, k : k + 1, :]).astype(jnp.float32)
            pcol[k, j * elements : (j + 1) * elements, :] = jnp.broadcast_to(line, (LANES, elements)).T

    spread_positions(0)
    for j in range(1, 4):
        pos_copies[j - 1].wait_recv()
        spread_positions(j)
    row_copies[2].start()
    pltpu.make_async_copy(ang, ang, ang_recv).wait()

    def steer(j, first):
        @pl.loop(0, elements // CHUNK)
        def _(i):
            row = pl.multiple_of(i * CHUNK, CHUNK)
            p0 = pcol[0, pl.ds(j * elements + row, CHUNK), :]
            p1 = pcol[1, pl.ds(j * elements + row, CHUNK), :]
            for lane in range(0, angles, LANES):
                block = group * blocks + first + lane // per_block
                inner = lane % per_block
                a = ang[block, :, inner : inner + LANES].astype(jnp.float32) * (1.0 / PHASES)
                cos, sin = cos_sin(p0 * a[0:1] + p1 * a[1:2])
                steering[j, pl.ds(row, CHUNK), lane : lane + LANES] = cos.astype(jnp.bfloat16)
                steering[j, pl.ds(row, CHUNK), angles + lane : angles + lane + LANES] = sin.astype(jnp.bfloat16)

    def project(j):
        left = v[j].reshape(4 * width, elements)
        for tile in range(0, 2 * angles, TILE):
            product = jnp.dot(left, steering[j, :, tile : tile + TILE], preferred_element_type=jnp.float32)
            if j == 0:
                acc[:, :, tile : tile + TILE] = product.reshape(2, 2 * width, TILE)
            else:
                acc[:, :, tile : tile + TILE] += product.reshape(2, 2 * width, TILE)

    counted = lax.broadcasted_iota(jnp.int32, (width, TILE), 0) >= shared * half

    def finish(which, first, add):
        left = v[3, which].reshape(2 * width, elements)
        for tile in range(0, angles, TILE):
            with_cos = acc[which, :, tile : tile + TILE] + jnp.dot(
                left, steering[3, :, tile : tile + TILE], preferred_element_type=jnp.float32)
            with_sin = acc[which, :, angles + tile : angles + tile + TILE] + jnp.dot(
                left, steering[3, :, angles + tile : angles + tile + TILE], preferred_element_type=jnp.float32)
            real = with_cos[:width] + with_sin[width:]
            imag = with_sin[:width] - with_cos[width:]
            power = jnp.where(counted, real * real + imag * imag, 0.0)
            total = jnp.sum(power, axis=0, keepdims=True)
            block, inner = first + tile // per_block, tile % per_block
            if add:
                total = total + part[block, :, inner : inner + TILE]
            part[block, :, inner : inner + TILE] = total

    for first in range(0, blocks, angles // per_block):
        opening = first == 0
        steer(0, first)
        steer(1, first)
        if opening:
            for j in (1, 2):
                row_copies[j - 1].wait_recv()
                core_copies[j].start()
            own_copy.wait()
            core_copies[0].wait_recv()
        project(0)
        steer(2, first)
        steer(3, first)
        for j in (1, 2):
            if opening:
                core_copies[j].wait_recv()
            project(j)
        if opening:
            row_copies[2].wait_recv()
            core_copies[3].start()
        finish(core, first, False)
        if opening:
            core_copies[3].wait_recv()
        finish(1 - core, first, True)

    slot = half * (grid // 2) + chip
    transfers = []
    for i in range(blocks):
        for row in range(4):
            target = group * blocks + i
            here = jnp.logical_and(target == g, r == row)
            index = i * 4 + row
            remote = pltpu.make_async_remote_copy(
                part.at[i], red.at[slot], red_send.at[index], red_recv.at[slot],
                device_id=(row, target), device_id_type=MESH)
            local = pltpu.make_async_copy(part.at[i], red.at[slot], red_recv.at[slot])
            transfers.append((here, remote))
            pl.when(here)(local.start)
            pl.when(jnp.logical_not(here))(remote.start)
    for s in range(grid):
        pltpu.make_async_copy(part.at[0], red.at[s], red_recv.at[s]).wait()
    squares = red[0]
    for s in range(1, grid):
        squares = squares + red[s]
    out_ref[...] = 1.0 / (squares / noise + LOADING)

    for here, remote in transfers:
        pl.when(jnp.logical_not(here))(remote.wait_send)
    for copy in pos_copies + row_copies + core_copies:
        copy.wait_send()
    others = ang.at[pl.ds(0, grid - 1)]
    pltpu.make_async_copy(others, others, ang_send).wait()


def body(grid, positions, angles, subspace):
    parts, elements, columns = subspace.shape
    stored = SUBLANES * pl.cdiv(columns, SUBLANES)
    width = SUBLANES * pl.cdiv(stored, 2 * SUBLANES)
    by_column = jnp.swapaxes(subspace, 1, 2)
    if stored > columns:
        by_column = jnp.pad(by_column, ((0, 0), (0, stored - columns), (0, 0)))
    per_block = angles.shape[1]
    blocks = grid // 4
    span = min(SPAN, blocks) * per_block
    noise = columns * grid
    dma = pltpu.SemaphoreType.DMA
    out = pl.pallas_call(
        functools.partial(kernel, grid, noise),
        out_shape=jax.ShapeDtypeStruct((1, per_block), jnp.float32),
        in_specs=[
            pl.BlockSpec(memory_space=pltpu.VMEM),
            pl.BlockSpec(memory_space=pltpu.VMEM),
            pl.BlockSpec(memory_space=pl.ANY),
        ],
        out_specs=pl.BlockSpec(memory_space=pltpu.VMEM),
        scratch_shapes=[
            pltpu.VMEM((4, 2, elements), jnp.int32),
            pltpu.VMEM((grid, 2, per_block), jnp.int32),
            pltpu.VMEM((2, 4 * elements, LANES), jnp.float32),
            pltpu.VMEM((4, 2, 2, width, elements), jnp.bfloat16),
            pltpu.VMEM((4, elements, 2 * span), jnp.bfloat16),
            pltpu.VMEM((2, 2 * width, 2 * span), jnp.float32),
            pltpu.VMEM((blocks, 1, per_block), jnp.float32),
            pltpu.VMEM((grid, 1, per_block), jnp.float32),
            dma, dma, dma((4,)), dma((4,)), dma,
            dma((4,)), dma((4,)), dma((4,)), dma((4,)), dma((4 * blocks,)), dma((grid,)),
        ],
        compiler_params=pltpu.CompilerParams(collective_id=0, has_side_effects=True),
    )(positions, angles, by_column)
    return out.reshape(per_block)


def solution(mesh):
    in_specs = (P(None, "rows"), P(None, "grid"), P(None, "rows", "grid"))
    fn = functools.partial(body, mesh.shape["grid"])
    return jax.shard_map(fn, mesh=mesh, in_specs=in_specs, out_specs=P("grid"), check_vma=False)
```

time: 34.3 us -> 30.7 us (0.90)
  local copies, waits for them, and re-layouts: 3.32 us -> 1.26 us
  Pallas kernels: 30.7 us -> 29.2 us
    pallas_call x1, Pallas kernels: 30.7 us -> 29.2 us  [body(): pl.pallas_call(functools.partial(kernel, grid, noise), out_shape=jax.Shap...]
    pad x1 -> x0, local copies, waits for them, and re-layouts: 1.06 us -> none  [body(): padded = jnp.pad(subspace, ((0, 0), (0, 0), (0, 2 * width - columns)))]
    reshape x1 -> x0, local copies, waits for them, and re-layouts: 1 us -> none  [body(): halves = jnp.moveaxis(padded.reshape(parts, elements, 2, width), 2, 0)]
where the time goes in v2:
time: 30.7 us; the launch traced here: 30.4 us
  Pallas kernels  29.2 us (95%)
  local copies, waits for them, and re-layouts  1.26 us (4%)
    pallas_call x1, Pallas kernels, body(): pl.pallas_call(functools.partial(kernel, grid, noise), out_shape=jax.Shap...  29.2 us
    unnamed x1, local copies, waits for them, and re-layouts  1.26 us

profile of v2, /device:TPU:0, one launch (start us, length us, event | category | flops | bytes accessed | tf_op | source)
XLA Modules:
  0.0 30.4 jit_solution(3189360892991960884)
XLA Ops:
  0.0 29.2 %shard_map.37 = f32[1,512]{1,0:T(1,128)} custom-call(s32[2,512]{1,0:T(2,128)} %pos_ref.1, s32[2,512]{1,0:T(2,128)} %ang_ref.1, bf16[2,240,512]{2,1,0:T(8,128)(2,1)} %bitcast.2), custom_call_target="tpu_custom_call" | custom-call | tf_op jit(solution)/shard_map/pallas_call | solution.py:237
  29.2 1.3 %copy.5 = f32[512]{0:T(512)} copy(f32[512]{0:T(512)} %bitcast.3) | data formatting | bytes 4096

commit v3 on v2

--- a/solution.py
+++ b/solution.py
@@ -13,7 +13,7 @@
 LANES = 128
 SUBLANES = 16
 TILE = 256
-CHUNK = 32
+CHUNK = 64
 SPAN = 2
 
 COS_ODD = (-6.283164024353027, 41.33714294433594, -81.34076690673828, 70.9933853149414)
@@ -48,10 +48,11 @@
 
 def kernel(
     grid, noise, pos_ref, ang_ref, v_ref, out_ref,
-    pos, ang, pcol, v, steering, acc, part, red,
+    pos, ang, pcol, v, steering0, steering1, steering2, steering3, acc, part, red,
     ang_send, ang_recv, pos_send, pos_recv, own_sem,
     row_send, row_recv, core_send, core_recv, red_send, red_recv,
 ):
+    steering = (steering0, steering1, steering2, steering3)
     r, g = lax.axis_index("rows"), lax.axis_index("grid")
     half, y = r % 2, r // 2
     core, chip = g % 2, g // 2
@@ -62,7 +63,7 @@
     width = v.shape[3]
     stored = v_ref.shape[1]
     shared = 2 * width - stored
-    angles = steering.shape[2] // 2
+    angles = steering[0].shape[1] // 2
 
     def row_partner(j):
         return flip(y, j // 2) * 2 + flip(half, j % 2)
@@ -127,28 +128,36 @@
     row_copies[2].start()
     pltpu.make_async_copy(ang, ang, ang_recv).wait()
 
-    def steer(j, first):
-        @pl.loop(0, elements // CHUNK)
+    def steer_rows(j, first, row):
+        p0 = pcol[0, pl.ds(j * elements + row, CHUNK), :]
+        p1 = pcol[1, pl.ds(j * elements + row, CHUNK), :]
+        for lane in range(0, angles, LANES):
+            block = group * blocks + first + lane // per_block
+            inner = lane % per_block
+            a = ang[block, :, inner : inner + LANES].astype(jnp.float32) * (1.0 / PHASES)
+            cos, sin = cos_sin(p0 * a[0:1] + p1 * a[1:2])
+            steering[j][pl.ds(row, CHUNK), lane : lane + LANES] = cos.astype(jnp.bfloat16)
+            steering[j][pl.ds(row, CHUNK), angles + lane : angles + lane + LANES] = sin.astype(jnp.bfloat16)
+
+    def project_tile(j, start, size):
+        left = v[j].reshape(4 * width, elements)
+        columns = pl.ds(start, size)
+        product = jnp.dot(left, steering[j][:, columns], preferred_element_type=jnp.float32)
+        product = product.reshape(2, 2 * width, size)
+        if j == 0:
+            acc[:, :, columns] = product
+        else:
+            acc[:, :, columns] += product
+
+    chunks = elements // CHUNK
+    step = 2 * angles // chunks
+
+    def sweep(j, first, begin, end):
+        @pl.loop(begin, end)
         def _(i):
-            row = pl.multiple_of(i * CHUNK, CHUNK)
-            p0 = pcol[0, pl.ds(j * elements + row, CHUNK), :]
-            p1 = pcol[1, pl.ds(j * elements + row, CHUNK), :]
-            for lane in range(0, angles, LANES):
-                block = group * blocks + first + lane // per_block
-                inner = lane % per_block
-                a = ang[block, :, inner : inner + LANES].astype(jnp.float32) * (1.0 / PHASES)
-                cos, sin = cos_sin(p0 * a[0:1] + p1 * a[1:2])
-                steering[j, pl.ds(row, CHUNK), lane : lane + LANES] = cos.astype(jnp.bfloat16)
-                steering[j, pl.ds(row, CHUNK), angles + lane : angles + lane + LANES] = sin.astype(jnp.bfloat16)
-
-    def project(j):
-        left = v[j].reshape(4 * width, elements)
-        for tile in range(0, 2 * angles, TILE):
-            product = jnp.dot(left, steering[j, :, tile : tile + TILE], preferred_element_type=jnp.float32)
-            if j == 0:
-                acc[:, :, tile : tile + TILE] = product.reshape(2, 2 * width, TILE)
-            else:
-                acc[:, :, tile : tile + TILE] += product.reshape(2, 2 * width, TILE)
+            if j > 0:
+                project_tile(j - 1, pl.multiple_of(i * step, step), step)
+            steer_rows(j, first, pl.multiple_of(i * CHUNK, CHUNK))
 
     counted = lax.broadcasted_iota(jnp.int32, (width, TILE), 0) >= shared * half
 
@@ -156,9 +165,9 @@
         left = v[3, which].reshape(2 * width, elements)
         for tile in range(0, angles, TILE):
             with_cos = acc[which, :, tile : tile + TILE] + jnp.dot(
-                left, steering[3, :, tile : tile + TILE], preferred_element_type=jnp.float32)
+                left, steering[3][:, tile : tile + TILE], preferred_element_type=jnp.float32)
             with_sin = acc[which, :, angles + tile : angles + tile + TILE] + jnp.dot(
-                left, steering[3, :, angles + tile : angles + tile + TILE], preferred_element_type=jnp.float32)
+                left, steering[3][:, angles + tile : angles + tile + TILE], preferred_element_type=jnp.float32)
             real = with_cos[:width] + with_sin[width:]
             imag = with_sin[:width] - with_cos[width:]
             power = jnp.where(counted, real * real + imag * imag, 0.0)
@@ -170,24 +179,26 @@
 
     for first in range(0, blocks, angles // per_block):
         opening = first == 0
-        steer(0, first)
-        steer(1, first)
+        sweep(0, first, 0, chunks)
+        if opening:
+            own_copy.wait()
+            core_copies[0].wait_recv()
+        sweep(1, first, 0, 3 * chunks // 8)
         if opening:
             for j in (1, 2):
                 row_copies[j - 1].wait_recv()
                 core_copies[j].start()
-            own_copy.wait()
-            core_copies[0].wait_recv()
-        project(0)
-        steer(2, first)
-        steer(3, first)
-        for j in (1, 2):
-            if opening:
-                core_copies[j].wait_recv()
-            project(j)
+        sweep(1, first, 3 * chunks // 8, chunks)
+        if opening:
+            core_copies[1].wait_recv()
+        sweep(2, first, 0, chunks)
+        if opening:
+            core_copies[2].wait_recv()
+        sweep(3, first, 0, chunks // 2)
         if opening:
             row_copies[2].wait_recv()
             core_copies[3].start()
+        sweep(3, first, chunks // 2, chunks)
         finish(core, first, False)
         if opening:
             core_copies[3].wait_recv()
@@ -248,7 +259,7 @@
             pltpu.VMEM((grid, 2, per_block), jnp.int32),
             pltpu.VMEM((2, 4 * elements, LANES), jnp.float32),
             pltpu.VMEM((4, 2, 2, width, elements), jnp.bfloat16),
-            pltpu.VMEM((4, elements, 2 * span), jnp.bfloat16),
+            *[pltpu.VMEM((elements, 2 * span), jnp.bfloat16)] * 4,
             pltpu.VMEM((2, 2 * width, 2 * span), jnp.float32),
             pltpu.VMEM((blocks, 1, per_block), jnp.float32),
             pltpu.VMEM((grid, 1, per_block), jnp.float32),

time: 30.7 us -> 33.3 us (1.085)
  Pallas kernels: 29.2 us -> 31.8 us
    pallas_call x1, Pallas kernels: 29.2 us -> 31.8 us  [body(): pl.pallas_call(functools.partial(kernel, grid, noise), out_shape=jax.Shap...]
where the time goes in v3:
time: 33.3 us; the launch traced here: 33 us
  Pallas kernels  31.8 us (95%)
  local copies, waits for them, and re-layouts  1.26 us (4%)
    pallas_call x1, Pallas kernels, body(): pl.pallas_call(functools.partial(kernel, grid, noise), out_shape=jax.Shap...  31.8 us
    unnamed x1, local copies, waits for them, and re-layouts  1.26 us

profile of v3, /device:TPU:0, one launch (start us, length us, event | category | flops | bytes accessed | tf_op | source)
XLA Modules:
  0.0 33.0 jit_solution(15203682013640045483)
XLA Ops:
  0.0 31.8 %shard_map.37 = f32[1,512]{1,0:T(1,128)} custom-call(s32[2,512]{1,0:T(2,128)} %pos_ref.1, s32[2,512]{1,0:T(2,128)} %ang_ref.1, bf16[2,240,512]{2,1,0:T(8,128)(2,1)} %bitcast.2), custom_call_target="tpu_custom_call" | custom-call | tf_op jit(solution)/shard_map/pallas_call | solution.py:248
  31.8 1.3 %copy.5 = f32[512]{0:T(512)} copy(f32[512]{0:T(512)} %bitcast.3) | data formatting | bytes 4096
